TPU v7x, 32 devices: a whole 2x2x4 slice. The times are simulated.
32 devices in a mesh: dp: 8 (over z, x), seq: 4 (over y, core).
Axes of the slice: x: 2, y: 2, z: 4, core: 2. Of those that a mesh axis runs over, the one named last changes fastest.
Arguments:
- queries: bfloat16 [8, 512, 1024], P('dp', 'seq'), may hold values from -6 to 6
- key_vecs: bfloat16 [8, 512, 1024], P('dp', 'seq'), may hold values from -6 to 6
- value_vecs: bfloat16 [8, 512, 1024], P('dp', 'seq'), may hold values from -6 to 6
- residual_in: bfloat16 [8, 512, 1024], P('dp', 'seq'), may hold values from -8 to 8
- point_weight: bfloat16 [1024, 2048], P('seq'), may hold values from -0.5 to 0.5
- context_grad: bfloat16 [8, 512, 1024], P('dp', 'seq'), may hold values from -6 to 6
- depth_kernel: float32 [31, 1024], replicated, may hold values from -1 to 1
- norm_gain: float32 [1024], replicated, may hold values from 0.5 to 1.5
- norm_bias: float32 [1024], replicated, may hold values from -3 to 3
- conv_grad: bfloat16 [8, 512, 1024], P('dp', 'seq'), may hold values from -1.5 to 1.5
Outputs:
- context: bfloat16 [8, 512, 1024], P('dp', 'seq')
- conv_output: bfloat16 [8, 512, 1024], P('dp', 'seq')
- query_grad: bfloat16 [8, 512, 1024], P('dp', 'seq')
- key_grad: bfloat16 [8, 512, 1024], P('dp', 'seq')
- value_grad: bfloat16 [8, 512, 1024], P('dp', 'seq')
- input_grad: bfloat16 [8, 512, 2048], P('dp', 'seq')
- residual_grad: bfloat16 [8, 512, 1024], P('dp', 'seq')
- kernel_grad: float32 [31, 1024], replicated
- gain_grad: float32 [1024], replicated
- bias_grad: float32 [1024], replicated
All inputs are finite; a program needn't handle non-finite values.
Results may differ from a plain program's by a relative error of at most 0.0049.
The roundings to bfloat16 on the way count: a program that leaves them out, or rounds other values in their place, can miss the bound.
Values may be sent and summed in bfloat16 or wider, within the bound.
A program may use at most 64 MiB of HBM per device.

v0:
```python
import jax
import jax.numpy as jnp
from jax import lax
from jax.sharding import PartitionSpec as P

HEADS = 16


def from_behind(block, axis, distance):
    devices = range(lax.axis_size(axis))
    route = [(i - distance, i) for i in devices if i - distance in devices]
    return lax.ppermute(block, axis, route)


def block_probs(query_block, key_heads, scaling):
    scores = (
        jnp.einsum("qhd,khd->hqk", query_block, key_heads, preferred_element_type=jnp.float32)
        * scaling
    )
    shifted = jnp.exp(scores - jnp.max(scores, axis=2, keepdims=True))
    return shifted / jnp.sum(shifted, axis=2, keepdims=True)


def attend_forward(query_part, key_part, value_part, head_count):
    frames, channels = query_part.shape
    head_depth = channels // head_count
    scaling = head_depth ** (-0.5)
    query_heads = query_part.reshape(frames, head_count, head_depth)
    key_heads = key_part.reshape(frames, head_count, head_depth)
    value_heads = value_part.reshape(frames, head_count, head_depth)
    block_rows = min(512, frames)

    def one_block(running, index):
        query_block = lax.dynamic_slice_in_dim(query_heads, index * block_rows, block_rows, 0)
        rounded = block_probs(query_block, key_heads, scaling).astype(jnp.bfloat16)
        context = jnp.einsum(
            "hqk,khd->qhd", rounded, value_heads, preferred_element_type=jnp.float32
        ).astype(jnp.bfloat16)
        return (running, context)

    unused, blocks = lax.scan(
        one_block, jnp.zeros((), jnp.float32), jnp.arange(frames // block_rows)
    )
    return blocks.reshape(frames, channels)


def attend_backward(query_part, key_part, value_part, grad_part, context_part, head_count):
    frames, channels = query_part.shape
    head_depth = channels // head_count
    scaling = head_depth ** (-0.5)
    query_heads = query_part.reshape(frames, head_count, head_depth)
    key_heads = key_part.reshape(frames, head_count, head_depth)
    value_heads = value_part.reshape(frames, head_count, head_depth)
    grad_heads = grad_part.reshape(frames, head_count, head_depth)
    context_heads = context_part.reshape(frames, head_count, head_depth)
    block_rows = min(512, frames)

    def one_block(running, index):
        key_total, value_total = running
        start = index * block_rows
        query_block = lax.dynamic_slice_in_dim(query_heads, start, block_rows, 0)
        grad_block = lax.dynamic_slice_in_dim(grad_heads, start, block_rows, 0)
        context_block = lax.dynamic_slice_in_dim(context_heads, start, block_rows, 0)
        probabilities = block_probs(query_block, key_heads, scaling)
        rounded = probabilities.astype(jnp.bfloat16)
        row_dots = jnp.sum(
            grad_block.astype(jnp.float32) * context_block.astype(jnp.float32), axis=2
        )
        prob_grad = jnp.einsum(
            "qhd,khd->hqk", grad_block, value_heads, preferred_element_type=jnp.float32
        )
        score_grad = (probabilities * (prob_grad - row_dots.T[:, :, None]) * scaling).astype(
            jnp.bfloat16
        )
        query_grad = jnp.einsum(
            "hqk,khd->qhd", score_grad, key_heads, preferred_element_type=jnp.float32
        ).astype(jnp.bfloat16)
        key_total = key_total + jnp.einsum(
            "hqk,qhd->khd", score_grad, query_block, preferred_element_type=jnp.float32
        )
        value_total = value_total + jnp.einsum(
            "hqk,qhd->khd", rounded, grad_block, preferred_element_type=jnp.float32
        )
        return ((key_total, value_total), query_grad)

    empty = jnp.zeros((frames, head_count, head_depth), jnp.float32)
    totals, blocks = lax.scan(one_block, (empty, empty), jnp.arange(frames // block_rows))
    query_grad = blocks.reshape(frames, channels)
    key_grad = totals[0].astype(jnp.bfloat16).reshape(frames, channels)
    value_grad = totals[1].astype(jnp.bfloat16).reshape(frames, channels)
    return (query_grad, key_grad, value_grad)


def shards(
    queries,
    key_vecs,
    value_vecs,
    residual_in,
    point_weight,
    context_grad,
    depth_kernel,
    norm_gain,
    norm_bias,
    conv_grad,
):
    head_count = HEADS // lax.axis_size("seq")
    query_heads, key_heads, value_heads = (
        lax.all_to_all(queries, "seq", split_axis=2, concat_axis=1, tiled=True),
        lax.all_to_all(key_vecs, "seq", split_axis=2, concat_axis=1, tiled=True),
        lax.all_to_all(value_vecs, "seq", split_axis=2, concat_axis=1, tiled=True),
    )
    context_local = attend_forward(query_heads[0], key_heads[0], value_heads[0], head_count)
    context_out = lax.all_to_all(
        context_local[None], "seq", split_axis=1, concat_axis=2, tiled=True
    )
    taps = depth_kernel.shape[0]
    channels = depth_kernel.shape[1]
    span = taps - 1
    frames = residual_in.shape[1]
    mixed = (residual_in[0].astype(jnp.float32) + context_out[0].astype(jnp.float32)).astype(
        jnp.bfloat16
    )
    pre_conv = jnp.dot(
        mixed,
        lax.all_gather(point_weight, "seq", axis=0, tiled=True),
        preferred_element_type=jnp.float32,
    )
    conv_input = pre_conv.astype(jnp.bfloat16)[None]
    value_half = conv_input[:, :, :channels].astype(jnp.float32)
    gate_sig = jax.nn.sigmoid(conv_input[:, :, channels:].astype(jnp.float32))
    glu = (value_half * gate_sig).astype(jnp.bfloat16)
    earlier = from_behind(glu[:, frames - span :], "seq", 1)
    glu_wide = jnp.concatenate([earlier, glu], axis=1)
    glu_view = lax.optimization_barrier(glu_wide).astype(jnp.float32)
    depthwise = jnp.zeros((1, frames, channels), jnp.float32)
    for offset in range(taps):
        depthwise = depthwise + depth_kernel[offset] * glu_view[:, offset : offset + frames]
    average = jnp.mean(depthwise, axis=2, keepdims=True)
    centered = depthwise - average
    variance = jnp.mean(centered * centered, axis=2, keepdims=True)
    inverse = lax.rsqrt(variance + 1e-05)
    normed = centered * inverse
    affine = normed * norm_gain + norm_bias
    sig_affine = jax.nn.sigmoid(affine)
    conv_output = (affine * sig_affine).astype(jnp.bfloat16)
    affine_grad = conv_grad.astype(jnp.float32) * (sig_affine * (1.0 + affine * (1.0 - sig_affine)))
    gain_term = jnp.sum(affine_grad * normed, axis=(0, 1))
    bias_term = jnp.sum(affine_grad, axis=(0, 1))
    normed_grad = affine_grad * norm_gain
    depth_grad = inverse * (
        normed_grad
        - jnp.mean(normed_grad, axis=2, keepdims=True)
        - normed * jnp.mean(normed_grad * normed, axis=2, keepdims=True)
    )
    kernel_term = jnp.stack(
        [
            jnp.sum(depth_grad * glu_view[:, offset : offset + frames], axis=(0, 1))
            for offset in range(taps)
        ]
    )
    kernel_total, gain_total, bias_total = lax.psum(
        (kernel_term, gain_term, bias_term), ("dp", "seq")
    )
    recordings = lax.axis_size("dp")
    kernel_grad = kernel_total / recordings
    gain_grad = gain_total / recordings
    bias_grad = bias_total / recordings
    later = from_behind(depth_grad[:, :span], "seq", -1)
    grad_wide = jnp.concatenate([depth_grad, later], axis=1)
    glu_grad = jnp.zeros((1, frames, channels), jnp.float32)
    for offset in range(taps):
        begin = span - offset
        glu_grad = glu_grad + depth_kernel[offset] * grad_wide[:, begin : begin + frames]
    input_grad = jnp.concatenate(
        [glu_grad * gate_sig, glu_grad * value_half * gate_sig * (1.0 - gate_sig)], axis=2
    ).astype(jnp.bfloat16)
    slope_rows = input_grad[0]
    mixed_grad = jnp.einsum(
        "fc,dc->fd",
        slope_rows,
        lax.all_gather(point_weight, "seq", axis=0, tiled=True),
        preferred_element_type=jnp.float32,
    )
    residual_grad = (context_grad.astype(jnp.float32) + mixed_grad[None]).astype(jnp.bfloat16)
    grad_heads = lax.all_to_all(residual_grad, "seq", split_axis=2, concat_axis=1, tiled=True)
    query_grad, key_grad, value_grad = attend_backward(
        query_heads[0], key_heads[0], value_heads[0], grad_heads[0], context_local, head_count
    )
    query_out, key_out, value_out = (
        lax.all_to_all(query_grad[None], "seq", split_axis=1, concat_axis=2, tiled=True),
        lax.all_to_all(key_grad[None], "seq", split_axis=1, concat_axis=2, tiled=True),
        lax.all_to_all(value_grad[None], "seq", split_axis=1, concat_axis=2, tiled=True),
    )
    return (
        context_out,
        conv_output,
        query_out,
        key_out,
        value_out,
        input_grad,
        residual_grad,
        kernel_grad,
        gain_grad,
        bias_grad,
    )


def solution(mesh):
    in_specs = (
        P("dp", "seq", None),
        P("dp", "seq", None),
        P("dp", "seq", None),
        P("dp", "seq", None),
        P("seq", None),
        P("dp", "seq", None),
        P(),
        P(),
        P(),
        P("dp", "seq", None),
    )
    out_specs = (
        P("dp", "seq", None),
        P("dp", "seq", None),
        P("dp", "seq", None),
        P("dp", "seq", None),
        P("dp", "seq", None),
        P("dp", "seq", None),
        P("dp", "seq", None),
        P(),
        P(),
        P(),
    )
    return jax.shard_map(shards, mesh=mesh, in_specs=in_specs, out_specs=out_specs, check_vma=False)
```

profile of v0, /device:TPU:0, one launch (start us, length us, event | category | flops | bytes accessed | tf_op | source)
XLA Modules:
  0.0 264.9 jit_solution(9525014765251899373)
XLA Ops:
  7.9 1.3 copy.72
  9.8 2.3 reduce.5
  12.9 4.2 %all-to-all-start = ((bf16[4,2,16384]{2,1,0:T(2,128)(2,1)}), bf16[4,2,16384]{2,1,0:T(2,128)(2,1)S(1)}, u32[]{:S(2)}, u32[]{:S(2)}) async-start(bf16[4,2,16384]{2,1,0:T(2,128)(2,1)} %reshape.213), calls=%async_computation | async-start | bytes 524288 | tf_op jit(solution)/shard_map/all_to_all | solution.py:108
  17.1 1.3 copy.74
  18.4 2.3 reduce.6
  21.4 2.4 all-to-all-done
  23.9 3.4 %all-to-all-start.1 = ((bf16[4,2,16384]{2,1,0:T(2,128)(2,1)}), bf16[4,2,16384]{2,1,0:T(2,128)(2,1)S(1)}, u32[]{:S(2)}, u32[]{:S(2)}) async-start(bf16[4,2,16384]{2,1,0:T(2,128)(2,1)} %reshape.215), calls=%async_computation.1 | async-start | bytes 524288 | tf_op jit(solution)/shard_map/all_to_all | solution.py:109
  27.7 2.3 reduce.4
  30.7 5.7 %all-to-all-done.1 = bf16[4,2,16384]{2,1,0:T(2,128)(2,1)S(1)} async-done(((bf16[4,2,16384]{2,1,0:T(2,128)(2,1)}), bf16[4,2,16384]{2,1,0:T(2,128)(2,1)S(1)}, u32[]{:S(2)}, u32[]{:S(2)}) %all-to-all-start.1) | async-done | bytes 262176 | tf_op jit(solution)/shard_map/all_to_all | solution.py:109
  36.4 3.4 %all-to-all-start.2 = ((bf16[4,2,16384]{2,1,0:T(2,128)(2,1)}), bf16[4,2,16384]{2,1,0:T(2,128)(2,1)S(1)}, u32[]{:S(2)}, u32[]{:S(2)}) async-start(bf16[4,2,16384]{2,1,0:T(2,128)(2,1)} %reshape.211), calls=%async_computation.2 | async-start | bytes 524288 | tf_op jit(solution)/shard_map/all_to_all | solution.py:110
  42.0 7.0 %all-to-all-done.2 = bf16[4,2,16384]{2,1,0:T(2,128)(2,1)S(1)} async-done(((bf16[4,2,16384]{2,1,0:T(2,128)(2,1)}), bf16[4,2,16384]{2,1,0:T(2,128)(2,1)S(1)}, u32[]{:S(2)}, u32[]{:S(2)}) %all-to-all-start.2) | async-done | bytes 262176 | tf_op jit(solution)/shard_map/all_to_all | solution.py:110
  49.6 3.5 %fusion.114 = (f32[4,512]{1,0:T(4,128)S(1)}, f32[4,512,512]{1,2,0:T(8,128)}) fusion(bf16[512,4,64]{0,2,1:T(8,128)(2,1)S(1)} %reshape_squeeze.15, bf16[512,4,64]{0,2,1:T(8,128)(2,1)S(1)} %reshape_squeeze.16), kind=kOutput, calls=%fused_computation.236 | convolution fusion | flops 137363968 | bytes 4726784 | tf_op jit(solution)/shard_map/while/body/eval_jaxpr/sub | solution.py:20
  53.1 2.8 %fusion.6 = bf16[4,512,512]{1,2,0:T(8,128)(2,1)S(1)} fusion(f32[4,512,512]{1,2,0:T(8,128)} %get-tuple-element.138, f32[4,512]{1,0:T(4,128)S(1)} %get-tuple-element.137), kind=kLoop, calls=%fused_computation.38 | loop fusion | flops 2097152 | bytes 6299648 | tf_op jit(solution)/shard_map/while/body/eval_jaxpr/convert_element_type | solution.py:35
  56.8 2.3 reduce.7
  59.8 3.6 %all-to-all-start.3 = ((bf16[4,2,16384]{2,1,0:T(2,128)(2,1)}), bf16[4,2,16384]{2,1,0:T(2,128)(2,1)S(1)}, u32[]{:S(2)}, u32[]{:S(2)}) async-start(bf16[4,2,16384]{2,1,0:T(2,128)(2,1)} %reshape.217), calls=%async_computation.3 | async-start | bytes 524288 | tf_op jit(solution)/shard_map/all_to_all | solution.py:113
  64.2 5.1 %all-to-all-done.3 = bf16[4,2,16384]{2,1,0:T(2,128)(2,1)S(1)} async-done(((bf16[4,2,16384]{2,1,0:T(2,128)(2,1)}), bf16[4,2,16384]{2,1,0:T(2,128)(2,1)S(1)}, u32[]{:S(2)}, u32[]{:S(2)}) %all-to-all-start.3) | async-done | bytes 262176 | tf_op jit(solution)/shard_map/all_to_all | solution.py:113
  69.7 1.1 fusion.105
  70.8 2.9 %fusion.4 = bf16[1,128,2048]{2,1,0:T(8,128)(2,1)S(1)} fusion(bf16[128,1024]{0,1:T(8,128)(2,1)S(1)} %fusion.105, bf16[1024,2048]{1,0:T(8,128)(2,1)} %all-gather.2.cloned.1.call-done), kind=kOutput, calls=%fused_computation.35 | convolution fusion | flops 537133056 | bytes 4980736 | tf_op jit(solution)/shard_map/dot_general | solution.py:123
  74.5 2.2 collective-permute-start
  78.2 1.8 copy.95
  81.0 3.2 %fusion.111 = (f32[128]{0:T(128)S(1)}, f32[1,128,1024]{2,1,0:T(8,128)S(1)}) fusion(f32[1,158,1024]{2,1,0:T(8,128)S(1)} %convert_element_type.110, f32[1024]{0:T(1024)} %bitcast.253, f32[1024]{0:T(1024)} %bitcast.255, f32[1024]{0:T(1024)S(1)} %bitcast.197, f32[1024]{0:T(1024)S(1)} %bitcast.199, f32[1024]{0:T(1024)S(1)} %bitcast.201, f32[1024]{0:T(1024)} %bitcast.203, ...), kind=kLoop, calls=%fused_computation.233 | loop fusion | flops 8126336 | bytes 16904704 | tf_op jit(solution)/shard_map/reduce_sum | solution.py:138
  84.5 1.8 multiply_reduce_fusion.1
  86.2 1.3 multiply_reduce_fusion.2
  89.0 2.6 stack.127
  91.6 1.3 collective-permute-start.1
  92.9 43.4 %all-reduce = (f32[1024]{0:T(1024)}, f32[1024]{0:T(1024)}) all-reduce(f32[1024]{0:T(1024)} %get-tuple-element.93, f32[1024]{0:T(1024)} %get-tuple-element.96), channel_id=1, replica_groups=mesh['dp'=8,'seq'=4] {'dp','seq'}, use_global_device_ids=true, to_apply=%region_40.41 | all-reduce | flops 2048 | bytes 16384 | tf_op jit(solution)/shard_map/psum | solution.py:161
  136.3 1.3 broadcast_multiply_fusion.1
  137.6 3.6 %multiply_convert_fusion.1 = (bf16[1,128,1024]{2,1,0:T(8,128)(2,1)S(1)}, f32[1,128,1024]{2,1,0:T(8,128)S(1)}) fusion(bf16[1,128,2048]{2,1,0:T(8,128)(2,1)S(1)} %fusion.4, f32[1,128,1024]{2,1,0:T(8,128)S(1)} %get-tuple-element.99, f32[1024]{0:T(1024)} %bitcast.254, f32[1,30,1024]{2,1,0:T(8,128)S(1)} %collective-permute-done.1, f32[1024]{0:T(1024)} %bitcast.256, ...), kind=kLoop, calls=%fused_computation.210 | loop fusion | flops 12713984 | bytes 1822720 | tf_op jit(solution)/shard_map/convert.7
  141.9 3.7 %fusion.8 = bf16[1,128,1024]{2,1,0:T(8,128)(2,1)S(1)} fusion(bf16[1024,2048]{1,0:T(8,128)(2,1)} %all-gather.2.cloned.1.call-done, bf16[128,1024]{1,0:T(8,128)(2,1)S(1)} %bitcast.164, bf16[128,1024]{1,0:T(8,128)(2,1)S(1)} %bitcast.163, bf16[1,128,1024]{2,1,0:T(8,128)(2,1)} %param.15), kind=kOutput, calls=%fused_computation.74 | convolution fusion | flops 538312704 | bytes 5242880 | tf_op jit(solution)/shard_map/fc,dc->fd/dot_general | solution.py:178
  146.1 3.0 %reduce.8 = bf16[1024,128]{1,0:T(8,128)(2,1)} reduce(bf16[1024,1,128]{2,1,0:T(2,128)(2,1)S(1)} %bitcast.180, bf16[]{:T(256)} %broadcast.119), dimensions={1}, to_apply=%bitcast.135.reduce_sub_computation | reduce | bytes 524290
  149.0 1.7 reshape.219
  150.7 4.3 %all-to-all-start.4 = ((bf16[4,2,16384]{2,1,0:T(2,128)(2,1)}), bf16[4,2,16384]{2,1,0:T(2,128)(2,1)}, u32[]{:S(2)}, u32[]{:S(2)}) async-start(bf16[4,2,16384]{2,1,0:T(2,128)(2,1)} %reshape.219), calls=%async_computation.4 | async-start | bytes 524288 | tf_op jit(solution)/shard_map/all_to_all | solution.py:185
  155.0 61.4 %all-reduce.3.cloned.1.call-done = f32[31,1024]{1,0:T(8,128)} async-done(((f32[31,1024]{1,0:T(8,128)}), f32[31,1024]{1,0:T(8,128)}) %all-reduce.3.cloned.1.call-update) | async-done | bytes 126992 | tf_op jit(solution)/shard_map/psum | solution.py:161
  216.4 1.6 broadcast_multiply_fusion
  218.0 1.2 reshape.220
  219.5 1.5 convolution_convert_fusion.3
  221.1 3.1 %multiply_convert_fusion = bf16[4,512,512]{1,2,0:T(8,128)(2,1)S(1)} fusion(bf16[512,4,64]{0,2,1:T(8,128)(2,1)S(1)} %reshape_squeeze.18, bf16[512,4,64]{0,2,1:T(8,128)(2,1)S(1)} %copy-done.7, f32[4,512]{1,0:T(4,128)S(1)} %bitcast.288, f32[4,512,512]{1,2,0:T(8,128)} %get-tuple-element.138, f32[4,512]{1,0:T(4,128)S(1)} %copy-done.14), kind=kOutput, calls=%fused_computation.30 | convolution fusion | flops 139460608 | bytes 6832128 | tf_op jit(solution)/shard_map/while/body/eval_jaxpr/qhd,khd->hqk/dot_general | solution.py:69
  224.7 2.3 reduce.11
  227.7 4.0 %all-to-all-start.7 = ((bf16[4,2,16384]{2,1,0:T(2,128)(2,1)}), bf16[4,2,16384]{2,1,0:T(2,128)(2,1)}, u32[]{:S(2)}, u32[]{:S(2)}) async-start(bf16[4,2,16384]{2,1,0:T(2,128)(2,1)} %reshape.225), calls=%async_computation.7 | async-start | bytes 524288 | tf_op jit(solution)/shard_map/all_to_all | solution.py:192
  231.7 1.7 convolution_convert_fusion.4
  233.9 2.3 reduce.10
  237.8 3.4 %all-to-all-start.6 = ((bf16[4,2,16384]{2,1,0:T(2,128)(2,1)}), bf16[4,2,16384]{2,1,0:T(2,128)(2,1)S(1)}, u32[]{:S(2)}, u32[]{:S(2)}) async-start(bf16[4,2,16384]{2,1,0:T(2,128)(2,1)} %reshape.223), calls=%async_computation.6 | async-start | bytes 524288 | tf_op jit(solution)/shard_map/all_to_all | solution.py:191
  241.2 1.4 convolution_convert_fusion.1
  243.1 2.3 reduce.9
  246.1 1.1 all-to-all-done.6
  247.3 3.4 %all-to-all-start.5 = ((bf16[4,2,16384]{2,1,0:T(2,128)(2,1)}), bf16[4,2,16384]{2,1,0:T(2,128)(2,1)S(1)}, u32[]{:S(2)}, u32[]{:S(2)}) async-start(bf16[4,2,16384]{2,1,0:T(2,128)(2,1)} %reshape.221), calls=%async_computation.5 | async-start | bytes 524288 | tf_op jit(solution)/shard_map/all_to_all | solution.py:190
  251.5 1.2 reshape.226
  255.1 1.6 all-to-all-done.5
  (102 shorter events, 25.1 us)
Async XLA Ops:
  7.2 20.1 %copy-start.8 = (bf16[1,128,1024]{2,1,0:T(8,128)(2,1)S(1)}, bf16[1,128,1024]{2,1,0:T(8,128)(2,1)}, u32[]{:S(2)}) copy-start(bf16[1,128,1024]{2,1,0:T(8,128)(2,1)} %param.12) | copy-start | bytes 786436
  7.2 63.6 %all-gather.2.cloned.1.call-start = ((), (), s32[]{:S(2)}) async-start(), calls=%async_computation.8 | async-start | bytes 5242880 | tf_op jit(solution)/shard_map/all_gather | solution.py:125
  7.9 31.9 %copy-start.10 = (bf16[1,128,1024]{2,1,0:T(8,128)(2,1)S(1)}, bf16[1,128,1024]{2,1,0:T(8,128)(2,1)}, u32[]{:S(2)}) copy-start(bf16[1,128,1024]{2,1,0:T(8,128)(2,1)} %param.13) | copy-start | bytes 786436
  12.9 11.0 %all-to-all-start = ((bf16[4,2,16384]{2,1,0:T(2,128)(2,1)}), bf16[4,2,16384]{2,1,0:T(2,128)(2,1)S(1)}, u32[]{:S(2)}, u32[]{:S(2)}) async-start(bf16[4,2,16384]{2,1,0:T(2,128)(2,1)} %reshape.213), calls=%async_computation | async-start | bytes 524288 | tf_op jit(solution)/shard_map/all_to_all | solution.py:108
  23.9 12.5 %all-to-all-start.1 = ((bf16[4,2,16384]{2,1,0:T(2,128)(2,1)}), bf16[4,2,16384]{2,1,0:T(2,128)(2,1)S(1)}, u32[]{:S(2)}, u32[]{:S(2)}) async-start(bf16[4,2,16384]{2,1,0:T(2,128)(2,1)} %reshape.215), calls=%async_computation.1 | async-start | bytes 524288 | tf_op jit(solution)/shard_map/all_to_all | solution.py:109
  36.4 12.5 %all-to-all-start.2 = ((bf16[4,2,16384]{2,1,0:T(2,128)(2,1)}), bf16[4,2,16384]{2,1,0:T(2,128)(2,1)S(1)}, u32[]{:S(2)}, u32[]{:S(2)}) async-start(bf16[4,2,16384]{2,1,0:T(2,128)(2,1)} %reshape.211), calls=%async_computation.2 | async-start | bytes 524288 | tf_op jit(solution)/shard_map/all_to_all | solution.py:110
  41.3 11.8 %copy-start.5 = (bf16[512,4,64]{0,2,1:T(8,128)(2,1)}, bf16[512,4,64]{0,2,1:T(8,128)(2,1)S(1)}, u32[]{:S(2)}) copy-start(bf16[512,4,64]{0,2,1:T(8,128)(2,1)S(1)} %reshape_squeeze.15) | copy-start | bytes 786436
  42.0 11.1 %copy-start.4 = (bf16[512,4,64]{0,2,1:T(8,128)(2,1)}, bf16[512,4,64]{0,2,1:T(8,128)(2,1)S(1)}, u32[]{:S(2)}) copy-start(bf16[512,4,64]{0,2,1:T(8,128)(2,1)S(1)} %reshape_squeeze.16) | copy-start | bytes 786436
  49.6 6.3 %copy-start.6 = (bf16[512,4,64]{0,2,1:T(8,128)(2,1)}, bf16[512,4,64]{0,2,1:T(8,128)(2,1)S(1)}, u32[]{:S(2)}) copy-start(bf16[512,4,64]{0,2,1:T(8,128)(2,1)S(1)} %reshape_squeeze.17) | copy-start | bytes 786436
  53.1 3.3 %copy-start.13 = (f32[4,512]{1,0:T(4,128)}, f32[4,512]{1,0:T(4,128)S(1)}, u32[]{:S(2)}) copy-start(f32[4,512]{1,0:T(4,128)S(1)} %get-tuple-element.137) | copy-start | bytes 24580
  55.9 7.6 %copy-start.11 = (f32[31,1024]{1,0:T(8,128)S(1)}, f32[31,1024]{1,0:T(8,128)}, u32[]{:S(2)}) copy-start(f32[31,1024]{1,0:T(8,128)} %param.16) | copy-start | bytes 380932
  59.8 9.4 %all-to-all-start.3 = ((bf16[4,2,16384]{2,1,0:T(2,128)(2,1)}), bf16[4,2,16384]{2,1,0:T(2,128)(2,1)S(1)}, u32[]{:S(2)}, u32[]{:S(2)}) async-start(bf16[4,2,16384]{2,1,0:T(2,128)(2,1)} %reshape.217), calls=%async_computation.3 | async-start | bytes 524288 | tf_op jit(solution)/shard_map/all_to_all | solution.py:113
  63.4 153.0 %all-reduce.3.cloned.1.call-start = ((), (), s32[]{:S(2)}) async-start(), calls=%async_computation.9 | async-start | bytes 262144 | tf_op jit(solution)/shard_map/psum | solution.py:161
  74.5 5.4 %collective-permute-start = (bf16[1,30,1024]{2,1,0:T(8,128)(2,1)}, bf16[1,30,1024]{2,1,0:T(8,128)(2,1)}, u32[]{:S(2)}, u32[]{:S(2)}) collective-permute-start(bf16[1,30,1024]{2,1,0:T(8,128)(2,1)} %slice.448), channel_id=1, source_target_pairs={{0,1},{1,2},{2,3},{4,5},{5,6},{6,7},{8,9},{9,10},{10,11},{12,13},{... | collective-permute-start | bytes 184328 | tf_op jit(solution)/shard_map/ppermute | solution.py:12
  80.9 3.5 %copy-start.9 = (bf16[1,128,1024]{2,1,0:T(8,128)(2,1)S(1)}, bf16[1,128,1024]{2,1,0:T(8,128)(2,1)}, u32[]{:S(2)}) copy-start(bf16[1,128,1024]{2,1,0:T(8,128)(2,1)} %param.19) | copy-start | bytes 786436
  81.0 3.5 %copy-start.12 = (f32[1024]{0:T(1024)S(1)}, f32[1024]{0:T(1024)}, u32[]{:S(2)}) copy-start(f32[1024]{0:T(1024)} %param.17) | copy-start | bytes 12292
  81.0 3.5 %copy-start.15 = (f32[1024]{0:T(1024)S(1)}, f32[1024]{0:T(1024)}, u32[]{:S(2)}) copy-start(f32[1024]{0:T(1024)} %param.18) | copy-start | bytes 12292
  91.6 46.0 %collective-permute-start.1 = (f32[1,30,1024]{2,1,0:T(8,128)}, f32[1,30,1024]{2,1,0:T(8,128)S(1)}, u32[]{:S(2)}, u32[]{:S(2)}) collective-permute-start(f32[1,30,1024]{2,1,0:T(8,128)} %slice.480), channel_id=1, source_target_pairs={{1,0},{2,1},{3,2},{5,4},{6,5},{7,6},{9,8},{10,9},{11,10},{13,12},{... | collective-permute-start | bytes 368648 | tf_op jit(solution)/shard_map/ppermute | solution.py:12
  141.2 0.7 copy-start
  145.6 73.6 %copy-start.2 = (bf16[1,128,1024]{2,1,0:T(8,128)(2,1)}, bf16[1,128,1024]{2,1,0:T(8,128)(2,1)S(1)}, u32[]{:S(2)}) copy-start(bf16[1,128,1024]{2,1,0:T(8,128)(2,1)S(1)} %fusion.8) | copy-start | bytes 786436
  145.7 75.4 %copy-start.14 = (f32[4,512]{1,0:T(4,128)S(1)}, f32[4,512]{1,0:T(4,128)}, u32[]{:S(2)}) copy-start(f32[4,512]{1,0:T(4,128)} %copy-done.13) | copy-start | bytes 24580
  150.7 67.2 %all-to-all-start.4 = ((bf16[4,2,16384]{2,1,0:T(2,128)(2,1)}), bf16[4,2,16384]{2,1,0:T(2,128)(2,1)}, u32[]{:S(2)}, u32[]{:S(2)}) async-start(bf16[4,2,16384]{2,1,0:T(2,128)(2,1)} %reshape.219), calls=%async_computation.4 | async-start | bytes 524288 | tf_op jit(solution)/shard_map/all_to_all | solution.py:185
  219.2 1.9 copy-start.7
  221.1 3.1 %copy-start.3 = (bf16[4,64,512]{2,1,0:T(8,128)(2,1)S(1)}, bf16[4,64,512]{2,1,0:T(8,128)(2,1)}, u32[]{:S(2)}) copy-start(bf16[4,64,512]{2,1,0:T(8,128)(2,1)} %convolution_convert_fusion.3) | copy-start | bytes 786436
  227.7 10.1 %all-to-all-start.7 = ((bf16[4,2,16384]{2,1,0:T(2,128)(2,1)}), bf16[4,2,16384]{2,1,0:T(2,128)(2,1)}, u32[]{:S(2)}, u32[]{:S(2)}) async-start(bf16[4,2,16384]{2,1,0:T(2,128)(2,1)} %reshape.225), calls=%async_computation.7 | async-start | bytes 524288 | tf_op jit(solution)/shard_map/all_to_all | solution.py:192
  233.4 17.2 %copy-start.1 = (bf16[1,128,1024]{2,1,0:T(8,128)(2,1)S(1)}, bf16[1,128,1024]{2,1,0:T(8,128)(2,1)}, u32[]{:S(2)}) copy-start(bf16[1,128,1024]{2,1,0:T(8,128)(2,1)} %copy-done) | copy-start | bytes 786436
  237.8 9.4 %all-to-all-start.6 = ((bf16[4,2,16384]{2,1,0:T(2,128)(2,1)}), bf16[4,2,16384]{2,1,0:T(2,128)(2,1)S(1)}, u32[]{:S(2)}, u32[]{:S(2)}) async-start(bf16[4,2,16384]{2,1,0:T(2,128)(2,1)} %reshape.223), calls=%async_computation.6 | async-start | bytes 524288 | tf_op jit(solution)/shard_map/all_to_all | solution.py:191
  247.3 9.4 %all-to-all-start.5 = ((bf16[4,2,16384]{2,1,0:T(2,128)(2,1)}), bf16[4,2,16384]{2,1,0:T(2,128)(2,1)S(1)}, u32[]{:S(2)}, u32[]{:S(2)}) async-start(bf16[4,2,16384]{2,1,0:T(2,128)(2,1)} %reshape.221), calls=%async_computation.5 | async-start | bytes 524288 | tf_op jit(solution)/shard_map/all_to_all | solution.py:190
Sparse Core Ops, SparseCore 0:
  9.6 43.2 all-gather.1
  91.7 124.6 all-reduce.2
where the time goes:
time: 266 us; the launch traced here: 265 us
  waiting for transfers between devices  85.9 us (32%)
  blocking collectives  43.4 us (16%)
  other arithmetic  38.5 us (14%)
  starting transfers between devices  33.3 us (13%)
  local copies, waits for them, and re-layouts  30.8 us (12%)
  matrix products  18.3 us (7%)
  between operations  14.8 us (6%)
    psum x1, waiting for transfers between devices, shards(): lax.psum((kernel_term, gain_term, bias_term), ('dp', 'seq'))  61.4 us
    psum x1, blocking collectives, shards(): lax.psum((kernel_term, gain_term, bias_term), ('dp', 'seq'))  43.4 us
    unnamed x65, local copies, waits for them, and re-layouts  20.7 us
    unnamed x8, other arithmetic  18.7 us
    all_to_all x1, waiting for transfers between devices, shards(): lax.all_to_all(value_vecs, 'seq', split_axis=2, concat_axis=1, tiled=True)  6.95 us
    all_to_all x1, waiting for transfers between devices, shards(): lax.all_to_all(key_vecs, 'seq', split_axis=2, concat_axis=1, tiled=True)  5.69 us
  transfers between devices with their start and end apart: 12, of which 8 were waited for; matrix products, arithmetic and copies ran while one was open for 23% of the time, Pallas kernels for 0%

commit v1 on v0

--- a/solution.py
+++ b/solution.py
@@ -159,7 +159,7 @@
         ]
     )
     kernel_total, gain_total, bias_total = lax.psum(
-        (kernel_term, gain_term, bias_term), ("dp", "seq")
+        lax.psum((kernel_term, gain_term, bias_term), "seq"), "dp"
     )
     recordings = lax.axis_size("dp")
     kernel_grad = kernel_total / recordings

time: 266 us -> 214 us (0.80)
  waiting for transfers between devices: 85.9 us -> 46.1 us
  blocking collectives: 43.4 us -> 32.3 us
  matrix products: 18.3 us -> 15.6 us
    psum x1 -> x2, waiting for transfers between devices: 61.4 us -> 17 us  [the longest x1 17 us: shards(): lax.psum(lax.psum((kernel_term, gain_term, bias_term), 'seq'), 'dp')]
    psum x1 -> x2, blocking collectives: 43.4 us -> 32.3 us  [the longest x1 24.2 us: shards(): lax.psum(lax.psum((kernel_term, gain_term, bias_term), 'seq'), 'dp')]
    all_to_all x1, waiting for transfers between devices: 0.01 us -> 4.1 us  [shards(): lax.all_to_all(residual_grad, 'seq', split_axis=2, concat_axis=1, tiled=T...]
  transfers between devices with their start and end apart: 12 -> 13, of which waited for: 8 -> 8; matrix products, arithmetic and copies ran while one was open for 23% -> 32% of each run, Pallas kernels for 0% -> 0%
where the time goes in v1:
time: 214 us; the launch traced here: 213 us
  waiting for transfers between devices  46.1 us (22%)
  other arithmetic  39.5 us (18%)
  starting transfers between devices  33.3 us (16%)
  blocking collectives  32.3 us (15%)
  local copies, waits for them, and re-layouts  31.4 us (15%)
  matrix products  15.6 us (7%)
  between operations  14.5 us (7%)
    psum x1, blocking collectives, shards(): lax.psum(lax.psum((kernel_term, gain_term, bias_term), 'seq'), 'dp')  24.2 us
    unnamed x65, local copies, waits for them, and re-layouts  21.3 us
    unnamed x8, other arithmetic  18.7 us
    psum x1, waiting for transfers between devices, shards(): lax.psum(lax.psum((kernel_term, gain_term, bias_term), 'seq'), 'dp')  17 us
    psum x1, blocking collectives, shards(): lax.psum((kernel_term, gain_term, bias_term), 'seq')  8.02 us
    all_to_all x1, waiting for transfers between devices, shards(): lax.all_to_all(value_vecs, 'seq', split_axis=2, concat_axis=1, tiled=True)  6.95 us
    all_to_all x1, waiting for transfers between devices, shards(): lax.all_to_all(key_vecs, 'seq', split_axis=2, concat_axis=1, tiled=True)  5.69 us
    all_to_all x1, waiting for transfers between devices, shards(): lax.all_to_all(context_local[None], 'seq', split_axis=1, concat_axis=2, t...  5.27 us
  transfers between devices with their start and end apart: 13, of which 8 were waited for; matrix products, arithmetic and copies ran while one was open for 32% of the time, Pallas kernels for 0%

profile of v1, /device:TPU:0, one launch (start us, length us, event | category | flops | bytes accessed | tf_op | source)
XLA Modules:
  0.0 212.7 jit_solution(5227789238799344264)
XLA Ops:
  7.9 1.3 copy.72
  9.8 2.3 %reduce.5 = bf16[1024,128]{1,0:T(8,128)(2,1)S(1)} reduce(bf16[1024,1,128]{2,1,0:T(2,128)(2,1)S(1)} %bitcast.173, bf16[]{:T(256)} %broadcast.119), dimensions={1}, to_apply=%bitcast.129.reduce_sub_computation | reduce | bytes 524290
  12.9 4.2 %all-to-all-start = ((bf16[4,2,16384]{2,1,0:T(2,128)(2,1)}), bf16[4,2,16384]{2,1,0:T(2,128)(2,1)S(1)}, u32[]{:S(2)}, u32[]{:S(2)}) async-start(bf16[4,2,16384]{2,1,0:T(2,128)(2,1)} %reshape.213), calls=%async_computation | async-start | bytes 524288 | tf_op jit(solution)/shard_map/all_to_all | solution.py:108
  17.1 1.3 copy.74
  18.4 2.3 %reduce.6 = bf16[1024,128]{1,0:T(8,128)(2,1)S(1)} reduce(bf16[1024,1,128]{2,1,0:T(2,128)(2,1)S(1)} %bitcast.177, bf16[]{:T(256)} %broadcast.119), dimensions={1}, to_apply=%bitcast.131.reduce_sub_computation | reduce | bytes 524290
  21.4 2.4 %all-to-all-done = bf16[4,2,16384]{2,1,0:T(2,128)(2,1)S(1)} async-done(((bf16[4,2,16384]{2,1,0:T(2,128)(2,1)}), bf16[4,2,16384]{2,1,0:T(2,128)(2,1)S(1)}, u32[]{:S(2)}, u32[]{:S(2)}) %all-to-all-start) | async-done | bytes 262176 | tf_op jit(solution)/shard_map/all_to_all | solution.py:108
  23.9 3.4 %all-to-all-start.1 = ((bf16[4,2,16384]{2,1,0:T(2,128)(2,1)}), bf16[4,2,16384]{2,1,0:T(2,128)(2,1)S(1)}, u32[]{:S(2)}, u32[]{:S(2)}) async-start(bf16[4,2,16384]{2,1,0:T(2,128)(2,1)} %reshape.215), calls=%async_computation.1 | async-start | bytes 524288 | tf_op jit(solution)/shard_map/all_to_all | solution.py:109
  27.7 2.3 %reduce.4 = bf16[1024,128]{1,0:T(8,128)(2,1)S(1)} reduce(bf16[1024,1,128]{2,1,0:T(2,128)(2,1)S(1)} %bitcast.178, bf16[]{:T(256)} %broadcast.119), dimensions={1}, to_apply=%bitcast.127.reduce_sub_computation | reduce | bytes 524290
  30.7 5.7 %all-to-all-done.1 = bf16[4,2,16384]{2,1,0:T(2,128)(2,1)S(1)} async-done(((bf16[4,2,16384]{2,1,0:T(2,128)(2,1)}), bf16[4,2,16384]{2,1,0:T(2,128)(2,1)S(1)}, u32[]{:S(2)}, u32[]{:S(2)}) %all-to-all-start.1) | async-done | bytes 262176 | tf_op jit(solution)/shard_map/all_to_all | solution.py:109
  36.4 3.4 %all-to-all-start.2 = ((bf16[4,2,16384]{2,1,0:T(2,128)(2,1)}), bf16[4,2,16384]{2,1,0:T(2,128)(2,1)S(1)}, u32[]{:S(2)}, u32[]{:S(2)}) async-start(bf16[4,2,16384]{2,1,0:T(2,128)(2,1)} %reshape.211), calls=%async_computation.2 | async-start | bytes 524288 | tf_op jit(solution)/shard_map/all_to_all | solution.py:110
  42.0 7.0 %all-to-all-done.2 = bf16[4,2,16384]{2,1,0:T(2,128)(2,1)S(1)} async-done(((bf16[4,2,16384]{2,1,0:T(2,128)(2,1)}), bf16[4,2,16384]{2,1,0:T(2,128)(2,1)S(1)}, u32[]{:S(2)}, u32[]{:S(2)}) %all-to-all-start.2) | async-done | bytes 262176 | tf_op jit(solution)/shard_map/all_to_all | solution.py:110
  49.6 3.5 %fusion.114 = (f32[4,512]{1,0:T(4,128)S(1)}, f32[4,512,512]{1,2,0:T(8,128)}) fusion(bf16[512,4,64]{0,2,1:T(8,128)(2,1)S(1)} %reshape_squeeze.15, bf16[512,4,64]{0,2,1:T(8,128)(2,1)S(1)} %reshape_squeeze.16), kind=kOutput, calls=%fused_computation.236 | convolution fusion | flops 137363968 | bytes 4726784 | tf_op jit(solution)/shard_map/while/body/eval_jaxpr/sub | solution.py:20
  53.7 2.8 %fusion.6 = bf16[4,512,512]{1,2,0:T(8,128)(2,1)S(1)} fusion(f32[4,512,512]{1,2,0:T(8,128)} %get-tuple-element.140, f32[4,512]{1,0:T(4,128)S(1)} %get-tuple-element.139), kind=kLoop, calls=%fused_computation.38 | loop fusion | flops 2097152 | bytes 6299648 | tf_op jit(solution)/shard_map/while/body/eval_jaxpr/convert_element_type | solution.py:35
  57.4 2.3 %reduce.7 = bf16[512,256]{1,0:T(8,128)(2,1)S(1)} reduce(bf16[512,1,256]{2,1,0:T(2,128)(2,1)S(1)} %bitcast.179, bf16[]{:T(256)} %broadcast.119), dimensions={1}, to_apply=%bitcast.133.reduce_sub_computation | reduce | bytes 524290
  60.4 3.6 %all-to-all-start.3 = ((bf16[4,2,16384]{2,1,0:T(2,128)(2,1)}), bf16[4,2,16384]{2,1,0:T(2,128)(2,1)S(1)}, u32[]{:S(2)}, u32[]{:S(2)}) async-start(bf16[4,2,16384]{2,1,0:T(2,128)(2,1)} %reshape.217), calls=%async_computation.3 | async-start | bytes 524288 | tf_op jit(solution)/shard_map/all_to_all | solution.py:113
  64.7 5.3 %all-to-all-done.3 = bf16[4,2,16384]{2,1,0:T(2,128)(2,1)S(1)} async-done(((bf16[4,2,16384]{2,1,0:T(2,128)(2,1)}), bf16[4,2,16384]{2,1,0:T(2,128)(2,1)S(1)}, u32[]{:S(2)}, u32[]{:S(2)}) %all-to-all-start.3) | async-done | bytes 262176 | tf_op jit(solution)/shard_map/all_to_all | solution.py:113
  70.5 1.1 fusion.105
  71.5 2.9 %fusion.4 = bf16[1,128,2048]{2,1,0:T(8,128)(2,1)S(1)} fusion(bf16[128,1024]{0,1:T(8,128)(2,1)S(1)} %fusion.105, bf16[1024,2048]{1,0:T(8,128)(2,1)} %all-gather.2.cloned.1.call-done), kind=kOutput, calls=%fused_computation.35 | convolution fusion | flops 537133056 | bytes 4980736 | tf_op jit(solution)/shard_map/dot_general | solution.py:123
  75.3 2.2 %collective-permute-start = (bf16[1,30,1024]{2,1,0:T(8,128)(2,1)}, bf16[1,30,1024]{2,1,0:T(8,128)(2,1)}, u32[]{:S(2)}, u32[]{:S(2)}) collective-permute-start(bf16[1,30,1024]{2,1,0:T(8,128)(2,1)} %slice.448), channel_id=1, source_target_pairs={{0,1},{1,2},{2,3},{4,5},{5,6},{6,7},{8,9},{9,10},{10,11},{12,13},{... | collective-permute-start | bytes 184328 | tf_op jit(solution)/shard_map/ppermute | solution.py:12
  78.9 1.8 copy.95
  81.7 3.2 %fusion.111 = (f32[128]{0:T(128)S(1)}, f32[1,128,1024]{2,1,0:T(8,128)S(1)}) fusion(f32[1,158,1024]{2,1,0:T(8,128)S(1)} %convert_element_type.110, f32[1024]{0:T(1024)} %bitcast.253, f32[1024]{0:T(1024)} %bitcast.255, f32[1024]{0:T(1024)S(1)} %bitcast.197, f32[1024]{0:T(1024)S(1)} %bitcast.199, f32[1024]{0:T(1024)S(1)} %bitcast.201, f32[1024]{0:T(1024)} %bitcast.203, ...), kind=kLoop, calls=%fused_computation.233 | loop fusion | flops 8126336 | bytes 16904704 | tf_op jit(solution)/shard_map/reduce_sum | solution.py:138
  85.2 1.8 multiply_reduce_fusion.1
  87.0 1.3 multiply_reduce_fusion.2
  89.7 2.7 %stack.127 = f32[31,1024]{1,0:T(8,128)} concatenate(f32[1,1024]{1,0:T(1,128)S(1)} %bitcast.287, f32[1,1024]{1,0:T(1,128)S(1)} %bitcast.286, f32[1,1024]{1,0:T(1,128)S(1)} %bitcast.285, f32[1,1024]{1,0:T(1,128)S(1)} %bitcast.284, f32[1,1024]{1,0:T(1,128)S(1)} %bitcast.283, f32[1,1024]{1,0:T(1,128)S(1)} %bitcast.282, f32[1,1024]{1,0:T(1,128)S(1)} %bitcast.281, ...), dimensions={0} | concatenate | bytes 253952 | tf_op jit(solution)/shard_map/stack | solution.py:155
  92.4 1.3 collective-permute-start.1
  93.7 8.0 %all-reduce.1 = (f32[1024]{0:T(1024)}, f32[1024]{0:T(1024)}) all-reduce(f32[1024]{0:T(1024)} %get-tuple-element.93, f32[1024]{0:T(1024)} %get-tuple-element.96), channel_id=1, replica_groups=mesh['dp'=8,'seq'=4] {'seq'}, use_global_device_ids=true, to_apply=%region_41.42 | all-reduce | flops 2048 | bytes 16384 | tf_op jit(solution)/shard_map/psum | solution.py:162
  101.8 24.2 %all-reduce = (f32[1024]{0:T(1024)}, f32[1024]{0:T(1024)}) all-reduce(f32[1024]{0:T(1024)} %get-tuple-element.99, f32[1024]{0:T(1024)} %get-tuple-element.100), channel_id=1, replica_groups=mesh['dp'=8,'seq'=4] {'dp'}, use_global_device_ids=true, to_apply=%region_42.43 | all-reduce | flops 2048 | bytes 16384 | tf_op jit(solution)/shard_map/psum | solution.py:161
  126.0 1.3 broadcast_multiply_fusion.1
  127.3 3.6 %multiply_convert_fusion.1 = (bf16[1,128,1024]{2,1,0:T(8,128)(2,1)S(1)}, f32[1,128,1024]{2,1,0:T(8,128)S(1)}) fusion(bf16[1,128,2048]{2,1,0:T(8,128)(2,1)S(1)} %fusion.4, f32[1,128,1024]{2,1,0:T(8,128)S(1)} %get-tuple-element.101, f32[1024]{0:T(1024)} %bitcast.254, f32[1,30,1024]{2,1,0:T(8,128)S(1)} %collective-permute-done.1, f32[1024]{0:T(1024)} %bitcast.256, ...), kind=kLoop, calls=%fused_computation.210 | loop fusion | flops 12713984 | bytes 1822720 | tf_op jit(solution)/shard_map/convert.7
  131.7 3.7 %fusion.8 = bf16[1,128,1024]{2,1,0:T(8,128)(2,1)S(1)} fusion(bf16[1024,2048]{1,0:T(8,128)(2,1)} %all-gather.2.cloned.1.call-done, bf16[128,1024]{1,0:T(8,128)(2,1)S(1)} %bitcast.164, bf16[128,1024]{1,0:T(8,128)(2,1)S(1)} %bitcast.163, bf16[1,128,1024]{2,1,0:T(8,128)(2,1)} %param.15), kind=kOutput, calls=%fused_computation.74 | convolution fusion | flops 538312704 | bytes 5242880 | tf_op jit(solution)/shard_map/fc,dc->fd/dot_general | solution.py:178
  135.8 3.0 %reduce.8 = bf16[1024,128]{1,0:T(8,128)(2,1)} reduce(bf16[1024,1,128]{2,1,0:T(2,128)(2,1)S(1)} %bitcast.180, bf16[]{:T(256)} %broadcast.119), dimensions={1}, to_apply=%bitcast.135.reduce_sub_computation | reduce | bytes 524290
  138.8 1.7 reshape.219
  140.5 4.3 %all-to-all-start.4 = ((bf16[4,2,16384]{2,1,0:T(2,128)(2,1)}), bf16[4,2,16384]{2,1,0:T(2,128)(2,1)}, u32[]{:S(2)}, u32[]{:S(2)}) async-start(bf16[4,2,16384]{2,1,0:T(2,128)(2,1)} %reshape.219), calls=%async_computation.4 | async-start | bytes 524288 | tf_op jit(solution)/shard_map/all_to_all | solution.py:185
  144.8 1.8 pad_maximum_fusion.1
  146.6 4.1 %all-to-all-done.4 = bf16[4,2,16384]{2,1,0:T(2,128)(2,1)} async-done(((bf16[4,2,16384]{2,1,0:T(2,128)(2,1)}), bf16[4,2,16384]{2,1,0:T(2,128)(2,1)}, u32[]{:S(2)}, u32[]{:S(2)}) %all-to-all-start.4) | async-done | bytes 262176 | tf_op jit(solution)/shard_map/all_to_all | solution.py:185
  150.7 1.2 reshape.220
  153.1 3.1 %multiply_convert_fusion = bf16[4,512,512]{1,2,0:T(8,128)(2,1)S(1)} fusion(bf16[512,4,64]{0,2,1:T(8,128)(2,1)S(1)} %reshape_squeeze.18, bf16[512,4,64]{0,2,1:T(8,128)(2,1)S(1)} %copy-done.7, f32[4,512]{1,0:T(4,128)S(1)} %bitcast.288, f32[4,512,512]{1,2,0:T(8,128)} %get-tuple-element.140, f32[4,512]{1,0:T(4,128)S(1)} %copy-done.14), kind=kOutput, calls=%fused_computation.30 | convolution fusion | flops 139460608 | bytes 6832128 | tf_op jit(solution)/shard_map/while/body/eval_jaxpr/qhd,khd->hqk/dot_general | solution.py:69
  156.6 2.3 %reduce.11 = bf16[512,256]{1,0:T(8,128)(2,1)S(1)} reduce(bf16[512,1,256]{2,1,0:T(2,128)(2,1)S(1)} %bitcast.175, bf16[]{:T(256)} %broadcast.119), dimensions={1}, to_apply=%bitcast.141.reduce_sub_computation | reduce | bytes 524290
  159.7 4.0 %all-to-all-start.7 = ((bf16[4,2,16384]{2,1,0:T(2,128)(2,1)}), bf16[4,2,16384]{2,1,0:T(2,128)(2,1)}, u32[]{:S(2)}, u32[]{:S(2)}) async-start(bf16[4,2,16384]{2,1,0:T(2,128)(2,1)} %reshape.225), calls=%async_computation.7 | async-start | bytes 524288 | tf_op jit(solution)/shard_map/all_to_all | solution.py:192
  164.9 2.3 %reduce.10 = bf16[512,256]{1,0:T(8,128)(2,1)S(1)} reduce(bf16[512,1,256]{2,1,0:T(2,128)(2,1)S(1)} %bitcast.176, bf16[]{:T(256)} %broadcast.119), dimensions={1}, to_apply=%bitcast.139.reduce_sub_computation | reduce | bytes 524290
  168.0 1.9 all-to-all-done.7
  169.8 3.4 %all-to-all-start.6 = ((bf16[4,2,16384]{2,1,0:T(2,128)(2,1)}), bf16[4,2,16384]{2,1,0:T(2,128)(2,1)S(1)}, u32[]{:S(2)}, u32[]{:S(2)}) async-start(bf16[4,2,16384]{2,1,0:T(2,128)(2,1)} %reshape.223), calls=%async_computation.6 | async-start | bytes 524288 | tf_op jit(solution)/shard_map/all_to_all | solution.py:191
  174.2 2.3 %reduce.9 = bf16[512,256]{1,0:T(8,128)(2,1)S(1)} reduce(bf16[512,1,256]{2,1,0:T(2,128)(2,1)S(1)} %bitcast.174, bf16[]{:T(256)} %broadcast.119), dimensions={1}, to_apply=%bitcast.137.reduce_sub_computation | reduce | bytes 524290
  177.2 2.1 all-to-all-done.6
  179.2 3.4 %all-to-all-start.5 = ((bf16[4,2,16384]{2,1,0:T(2,128)(2,1)}), bf16[4,2,16384]{2,1,0:T(2,128)(2,1)S(1)}, u32[]{:S(2)}, u32[]{:S(2)}) async-start(bf16[4,2,16384]{2,1,0:T(2,128)(2,1)} %reshape.221), calls=%async_computation.5 | async-start | bytes 524288 | tf_op jit(solution)/shard_map/all_to_all | solution.py:190
  182.7 17.0 %all-reduce.7.cloned.1.call-done = f32[31,1024]{1,0:T(8,128)} async-done(((f32[31,1024]{1,0:T(8,128)}), f32[31,1024]{1,0:T(8,128)}) %all-reduce.7.cloned.1.call-update) | async-done | bytes 126992 | tf_op jit(solution)/shard_map/psum | solution.py:161
  199.6 1.6 broadcast_multiply_fusion
  201.2 1.2 reshape.226
  (106 shorter events, 26.0 us)
Async XLA Ops:
  7.2 20.1 %copy-start.8 = (bf16[1,128,1024]{2,1,0:T(8,128)(2,1)S(1)}, bf16[1,128,1024]{2,1,0:T(8,128)(2,1)}, u32[]{:S(2)}) copy-start(bf16[1,128,1024]{2,1,0:T(8,128)(2,1)} %param.12) | copy-start | bytes 786436
  7.2 64.4 %all-gather.2.cloned.1.call-start = ((), (), s32[]{:S(2)}) async-start(), calls=%async_computation.8 | async-start | bytes 5242880 | tf_op jit(solution)/shard_map/all_gather | solution.py:125
  7.9 31.9 %copy-start.10 = (bf16[1,128,1024]{2,1,0:T(8,128)(2,1)S(1)}, bf16[1,128,1024]{2,1,0:T(8,128)(2,1)}, u32[]{:S(2)}) copy-start(bf16[1,128,1024]{2,1,0:T(8,128)(2,1)} %param.13) | copy-start | bytes 786436
  12.9 11.0 %all-to-all-start = ((bf16[4,2,16384]{2,1,0:T(2,128)(2,1)}), bf16[4,2,16384]{2,1,0:T(2,128)(2,1)S(1)}, u32[]{:S(2)}, u32[]{:S(2)}) async-start(bf16[4,2,16384]{2,1,0:T(2,128)(2,1)} %reshape.213), calls=%async_computation | async-start | bytes 524288 | tf_op jit(solution)/shard_map/all_to_all | solution.py:108
  23.9 12.5 %all-to-all-start.1 = ((bf16[4,2,16384]{2,1,0:T(2,128)(2,1)}), bf16[4,2,16384]{2,1,0:T(2,128)(2,1)S(1)}, u32[]{:S(2)}, u32[]{:S(2)}) async-start(bf16[4,2,16384]{2,1,0:T(2,128)(2,1)} %reshape.215), calls=%async_computation.1 | async-start | bytes 524288 | tf_op jit(solution)/shard_map/all_to_all | solution.py:109
  36.4 12.5 %all-to-all-start.2 = ((bf16[4,2,16384]{2,1,0:T(2,128)(2,1)}), bf16[4,2,16384]{2,1,0:T(2,128)(2,1)S(1)}, u32[]{:S(2)}, u32[]{:S(2)}) async-start(bf16[4,2,16384]{2,1,0:T(2,128)(2,1)} %reshape.211), calls=%async_computation.2 | async-start | bytes 524288 | tf_op jit(solution)/shard_map/all_to_all | solution.py:110
  41.3 11.8 %copy-start.4 = (bf16[512,4,64]{0,2,1:T(8,128)(2,1)}, bf16[512,4,64]{0,2,1:T(8,128)(2,1)S(1)}, u32[]{:S(2)}) copy-start(bf16[512,4,64]{0,2,1:T(8,128)(2,1)S(1)} %reshape_squeeze.15) | copy-start | bytes 786436
  42.0 11.1 %copy-start.2 = (bf16[512,4,64]{0,2,1:T(8,128)(2,1)}, bf16[512,4,64]{0,2,1:T(8,128)(2,1)S(1)}, u32[]{:S(2)}) copy-start(bf16[512,4,64]{0,2,1:T(8,128)(2,1)S(1)} %reshape_squeeze.16) | copy-start | bytes 786436
  49.6 6.9 %copy-start.6 = (bf16[512,4,64]{0,2,1:T(8,128)(2,1)}, bf16[512,4,64]{0,2,1:T(8,128)(2,1)S(1)}, u32[]{:S(2)}) copy-start(bf16[512,4,64]{0,2,1:T(8,128)(2,1)S(1)} %reshape_squeeze.17) | copy-start | bytes 786436
  53.1 0.6 copy-start.13
  56.5 7.6 %copy-start.11 = (f32[31,1024]{1,0:T(8,128)S(1)}, f32[31,1024]{1,0:T(8,128)}, u32[]{:S(2)}) copy-start(f32[31,1024]{1,0:T(8,128)} %param.16) | copy-start | bytes 380932
  60.4 9.6 %all-to-all-start.3 = ((bf16[4,2,16384]{2,1,0:T(2,128)(2,1)}), bf16[4,2,16384]{2,1,0:T(2,128)(2,1)S(1)}, u32[]{:S(2)}, u32[]{:S(2)}) async-start(bf16[4,2,16384]{2,1,0:T(2,128)(2,1)} %reshape.217), calls=%async_computation.3 | async-start | bytes 524288 | tf_op jit(solution)/shard_map/all_to_all | solution.py:113
  64.0 63.3 %all-reduce.5.cloned.1.call-start = ((), (), s32[]{:S(2)}) async-start(), calls=%async_computation.9 | async-start | bytes 262144 | tf_op jit(solution)/shard_map/psum | solution.py:162
  75.3 5.4 %collective-permute-start = (bf16[1,30,1024]{2,1,0:T(8,128)(2,1)}, bf16[1,30,1024]{2,1,0:T(8,128)(2,1)}, u32[]{:S(2)}, u32[]{:S(2)}) collective-permute-start(bf16[1,30,1024]{2,1,0:T(8,128)(2,1)} %slice.448), channel_id=1, source_target_pairs={{0,1},{1,2},{2,3},{4,5},{5,6},{6,7},{8,9},{9,10},{10,11},{12,13},{... | collective-permute-start | bytes 184328 | tf_op jit(solution)/shard_map/ppermute | solution.py:12
  81.7 3.5 %copy-start.9 = (bf16[1,128,1024]{2,1,0:T(8,128)(2,1)S(1)}, bf16[1,128,1024]{2,1,0:T(8,128)(2,1)}, u32[]{:S(2)}) copy-start(bf16[1,128,1024]{2,1,0:T(8,128)(2,1)} %param.19) | copy-start | bytes 786436
  81.7 3.5 %copy-start.12 = (f32[1024]{0:T(1024)S(1)}, f32[1024]{0:T(1024)}, u32[]{:S(2)}) copy-start(f32[1024]{0:T(1024)} %param.17) | copy-start | bytes 12292
  81.7 3.5 %copy-start.15 = (f32[1024]{0:T(1024)S(1)}, f32[1024]{0:T(1024)}, u32[]{:S(2)}) copy-start(f32[1024]{0:T(1024)} %param.18) | copy-start | bytes 12292
  92.4 107.2 %all-reduce.7.cloned.1.call-start = ((), (), s32[]{:S(2)}) async-start(), calls=%async_computation.10 | async-start | bytes 262144 | tf_op jit(solution)/shard_map/psum | solution.py:161
  92.4 34.9 %collective-permute-start.1 = (f32[1,30,1024]{2,1,0:T(8,128)}, f32[1,30,1024]{2,1,0:T(8,128)S(1)}, u32[]{:S(2)}, u32[]{:S(2)}) collective-permute-start(f32[1,30,1024]{2,1,0:T(8,128)} %slice.480), channel_id=1, source_target_pairs={{1,0},{2,1},{3,2},{5,4},{6,5},{7,6},{9,8},{10,9},{11,10},{13,12},{... | collective-permute-start | bytes 368648 | tf_op jit(solution)/shard_map/ppermute | solution.py:12
  131.0 0.7 copy-start
  135.4 17.6 %copy-start.1 = (bf16[1,128,1024]{2,1,0:T(8,128)(2,1)}, bf16[1,128,1024]{2,1,0:T(8,128)(2,1)S(1)}, u32[]{:S(2)}) copy-start(bf16[1,128,1024]{2,1,0:T(8,128)(2,1)S(1)} %fusion.8) | copy-start | bytes 786436
  135.8 17.3 %copy-start.14 = (f32[4,512]{1,0:T(4,128)S(1)}, f32[4,512]{1,0:T(4,128)}, u32[]{:S(2)}) copy-start(f32[4,512]{1,0:T(4,128)} %copy-done.13) | copy-start | bytes 24580
  140.5 10.2 %all-to-all-start.4 = ((bf16[4,2,16384]{2,1,0:T(2,128)(2,1)}), bf16[4,2,16384]{2,1,0:T(2,128)(2,1)}, u32[]{:S(2)}, u32[]{:S(2)}) async-start(bf16[4,2,16384]{2,1,0:T(2,128)(2,1)} %reshape.219), calls=%async_computation.4 | async-start | bytes 524288 | tf_op jit(solution)/shard_map/all_to_all | solution.py:185
  146.6 6.5 %copy-start.7 = (bf16[512,4,64]{0,2,1:T(8,128)(2,1)S(1)}, bf16[512,4,64]{0,2,1:T(8,128)(2,1)}, u32[]{:S(2)}) copy-start(bf16[512,4,64]{0,2,1:T(8,128)(2,1)} %copy-done.6) | copy-start | bytes 786436
  153.1 10.6 %copy-start.5 = (bf16[512,4,64]{0,2,1:T(8,128)(2,1)S(1)}, bf16[512,4,64]{0,2,1:T(8,128)(2,1)}, u32[]{:S(2)}) copy-start(bf16[512,4,64]{0,2,1:T(8,128)(2,1)} %copy-done.4) | copy-start | bytes 786436
  156.2 17.0 %copy-start.3 = (bf16[512,4,64]{0,2,1:T(8,128)(2,1)S(1)}, bf16[512,4,64]{0,2,1:T(8,128)(2,1)}, u32[]{:S(2)}) copy-start(bf16[512,4,64]{0,2,1:T(8,128)(2,1)} %copy-done.2) | copy-start | bytes 786436
  159.7 10.1 %all-to-all-start.7 = ((bf16[4,2,16384]{2,1,0:T(2,128)(2,1)}), bf16[4,2,16384]{2,1,0:T(2,128)(2,1)}, u32[]{:S(2)}, u32[]{:S(2)}) async-start(bf16[4,2,16384]{2,1,0:T(2,128)(2,1)} %reshape.225), calls=%async_computation.7 | async-start | bytes 524288 | tf_op jit(solution)/shard_map/all_to_all | solution.py:192
  169.8 9.4 %all-to-all-start.6 = ((bf16[4,2,16384]{2,1,0:T(2,128)(2,1)}), bf16[4,2,16384]{2,1,0:T(2,128)(2,1)S(1)}, u32[]{:S(2)}, u32[]{:S(2)}) async-start(bf16[4,2,16384]{2,1,0:T(2,128)(2,1)} %reshape.223), calls=%async_computation.6 | async-start | bytes 524288 | tf_op jit(solution)/shard_map/all_to_all | solution.py:191
  179.2 25.6 %all-to-all-start.5 = ((bf16[4,2,16384]{2,1,0:T(2,128)(2,1)}), bf16[4,2,16384]{2,1,0:T(2,128)(2,1)S(1)}, u32[]{:S(2)}, u32[]{:S(2)}) async-start(bf16[4,2,16384]{2,1,0:T(2,128)(2,1)} %reshape.221), calls=%async_computation.5 | async-start | bytes 524288 | tf_op jit(solution)/shard_map/all_to_all | solution.py:190
Sparse Core Ops, SparseCore 0:
  9.6 43.2 all-gather.1
  92.5 33.5 all-reduce.4
  129.9 69.6 all-reduce.6
